TPU v7x, 256 devices: a whole 4x4x8 slice. The times are simulated.
256 devices in a mesh: chain: 64 (over z, y, core), col: 4 (over x).
Axes of the slice: x: 4, y: 4, z: 8, core: 2. Of those that a mesh axis runs over, the one named last changes fastest.
Arguments:
- diagonal_blocks: float32 [192, 256, 256], P('chain', 'col'), may hold values from -2 to 6, as said below
- couplings: float32 [192, 256, 256], P('chain', 'col'), may hold values from -2 to 2
- right_sides: float32 [64, 192, 256], P('col', 'chain'), may hold values from -0.04 to 0.04
Outputs:
- solution: float32 [64, 192, 256], P('col', 'chain')
Inputs may be any that keep to these rules, and one draw needn't show every extreme that they name: `diagonal_blocks`: each block is symmetric, and the block-tridiagonal matrix that the diagonal blocks form with the couplings is positive definite with every eigenvalue 0.0003 or more.
All inputs are finite; a program needn't handle non-finite values.
Results may differ from a plain program's by a relative error of at most 0.0003.
Values sent between devices are 32-bit elements; how exact they have to be, the bound alone decides.
A program may use at most 64 MiB of HBM per device.

v0:
```python
import jax
import jax.numpy as jnp
from jax import lax
from jax.sharding import PartitionSpec as P

finest = lax.Precision.HIGHEST


def passed_along(shard, axis, by):
    size = lax.axis_size(axis)
    pairs = [(i, i + by) for i in range(size) if 0 <= i + by < size]
    return lax.ppermute(shard, axis, pairs)


def matmul(first_factor, second_factor):
    return jnp.dot(first_factor, second_factor, precision=finest)


def invert(matrix):
    lower_factor = jnp.linalg.cholesky(matrix)
    identity = jnp.eye(matrix.shape[0], dtype=matrix.dtype)
    return jax.scipy.linalg.cho_solve((lower_factor, True), identity)


def interior_solve(loads, inverses, products, inner_coups):
    before = jnp.concatenate([jnp.zeros_like(inner_coups), inner_coups], axis=0)

    def interior_forward(solved_prev, entries):
        load_now, coup_prev, inverse_now = entries
        reduced = load_now - matmul(solved_prev, coup_prev)
        solved_now = matmul(reduced, inverse_now.T)
        return (solved_now, solved_now)

    _, solved = lax.scan(interior_forward, jnp.zeros_like(loads[0]), (loads, before, inverses))

    def interior_backward(after, entries):
        solved_now, product = entries
        current = solved_now - matmul(after, product.T)
        return (current, current)

    _, earlier = lax.scan(interior_backward, solved[-1], (solved[:-1], products), reverse=True)
    return jnp.concatenate([earlier, solved[-1:]], axis=0)


def per_device(diagonal_blocks, couplings, right_sides):
    slab_count = diagonal_blocks.shape[0]
    col_width = diagonal_blocks.shape[1]
    inner_count = slab_count - 1
    col_start = lax.axis_index("col") * col_width
    chain_count = lax.axis_size("chain")
    levels = chain_count.bit_length() - 1
    full_diag, full_coup = (
        lax.all_gather(diagonal_blocks[:inner_count], "col", axis=1, tiled=True),
        lax.all_gather(couplings, "col", axis=1, tiled=True),
    )

    def body_forward(inverse_prev, entries):
        diag_now, coup_prev = entries
        product = matmul(inverse_prev, coup_prev)
        inverse_now = invert(diag_now - matmul(coup_prev.T, product))
        return (inverse_now, (inverse_prev, product))

    last_inverse, (early_inverses, products) = lax.scan(
        body_forward, invert(full_diag[0]), (full_diag[1:], full_coup[: inner_count - 1])
    )
    inverses = jnp.concatenate([early_inverses, last_inverse[None]], axis=0)
    inner_coups = full_coup[: inner_count - 1]
    coup_last = full_coup[inner_count - 1]
    coup_sep = full_coup[inner_count]
    last_cols = lax.dynamic_slice_in_dim(coup_last, col_start, col_width, 1)
    tail_start = matmul(last_inverse, last_cols)

    def body_backward(state, entries):
        green_block, tail_block = state
        inverse_now, product = entries
        green_block = inverse_now + matmul(matmul(product, green_block), product.T)
        tail_block = -matmul(product, tail_block)
        return ((green_block, tail_block), None)

    (near_green, near_tail), _ = lax.scan(
        body_backward, (last_inverse, tail_start), (early_inverses, products), reverse=True
    )
    loads = jnp.swapaxes(right_sides, 0, 1)
    interior = interior_solve(loads[:inner_count], inverses, products, inner_coups)
    got_green, got_tail, got_first = passed_along((near_green, near_tail, interior[0]), "chain", -1)
    sep_rows = lax.dynamic_slice_in_dim(coup_sep, col_start, col_width, 0)
    own_block = diagonal_blocks[inner_count].T
    b_part = (
        own_block
        - matmul(coup_last.T, tail_start)
        - matmul(coup_sep, matmul(got_green, sep_rows.T))
    )
    c_part = -matmul(coup_sep, got_tail)
    h_part = (
        loads[inner_count]
        - matmul(interior[inner_count - 1], coup_last)
        - matmul(got_first, coup_sep.T)
    )
    for level_index in range(levels):
        distance = 1 << level_index
        b_full, c_full = (
            lax.all_gather(b_part, "col", axis=1, tiled=True),
            lax.all_gather(c_part, "col", axis=1, tiled=True),
        )
        inverse = invert(b_full)
        coupling_rows = lax.dynamic_slice_in_dim(c_full, col_start, col_width, 0)
        solved_cols = matmul(inverse, c_part)
        solved_loads = matmul(h_part, inverse.T)
        below_blocks, below_loads = passed_along(
            (matmul(c_full.T, solved_cols), matmul(solved_loads, c_full)), "chain", distance
        )
        far_inverse, far_cols, far_loads = passed_along(
            (inverse, solved_cols, solved_loads), "chain", -distance
        )
        b_part = b_part - below_blocks - matmul(c_full, matmul(far_inverse, coupling_rows.T))
        c_part = -matmul(c_full, far_cols)
        h_part = h_part - below_loads - matmul(far_loads, c_full.T)
    b_final = lax.all_gather(b_part, "col", axis=1, tiled=True)
    separator = jax.scipy.linalg.cho_solve((jnp.linalg.cholesky(b_final), True), h_part.T).T
    carried = passed_along(matmul(separator, coup_sep), "chain", 1)
    adjusted = loads[:inner_count]
    adjusted = adjusted.at[0].add(-carried)
    adjusted = adjusted.at[inner_count - 1].add(-matmul(separator, coup_last.T))
    solved_inner = interior_solve(adjusted, inverses, products, inner_coups)
    return jnp.swapaxes(jnp.concatenate([solved_inner, separator[None]], axis=0), 0, 1)


def solution(mesh):
    in_specs = (P("chain", "col", None), P("chain", "col", None), P("col", "chain", None))
    out_specs = P("col", "chain", None)
    return jax.shard_map(
        per_device, mesh=mesh, in_specs=in_specs, out_specs=out_specs, check_vma=False
    )
```

profile of v0, /device:TPU:250, one launch (start us, length us, event | category | flops | bytes accessed | tf_op | source)
XLA Modules:
  0.0 923.8 jit_solution(14875295477138087786)
XLA Ops:
  1.0 13.5 %all_gather.45 = f32[2,256,256]{2,0,1:T(2,128)S(1)} all-gather(f32[2,64,256]{2,0,1:T(2,128)S(1)} %copy.26), channel_id=1, replica_groups=mesh['chain'=64,'col'=4] {'col'}, dimensions={1}, use_global_device_ids=true | all-gather | bytes 655360 | tf_op jit(solution)/shard_map/all_gather | solution.py:53
  37.2 11.7 %cholesky.441 = f32[128,128]{1,0:T(8,128)S(1)} custom-call(f32[128,128]{1,0:T(8,128)S(1)} %convolution_subtract_fusion.24), custom_call_target="Cholesky" | custom-call | tf_op jit(solution)/shard_map/jit(cholesky)/cholesky | solution.py:20
  55.0 19.7 %custom-call.37 = f32[2,128,128]{1,2,0:T(8,128)S(1)} custom-call(f32[2,128,128]{2,1,0:T(8,128)S(1)} %get-tuple-element.218), custom_call_target="InvertDiagBlocksLowerTriangular" | custom-call | tf_op jit(solution)/shard_map/jit(_cho_solve)/triangular_solve | solution.py:22
  77.1 14.0 %all_gather.46 = f32[3,256,256]{2,1,0:T(8,128)S(1)} all-gather(f32[3,64,256]{2,1,0:T(8,128)S(1)} %copy-done.19), channel_id=1, replica_groups=mesh['chain'=64,'col'=4] {'col'}, dimensions={1}, use_global_device_ids=true | all-gather | bytes 983040 | tf_op jit(solution)/shard_map/all_gather | solution.py:54
  115.3 11.7 %cholesky.475 = f32[128,128]{1,0:T(8,128)S(1)} custom-call(f32[128,128]{1,0:T(8,128)S(1)} %convolution_subtract_fusion.23), custom_call_target="Cholesky" | custom-call | tf_op jit(solution)/shard_map/while/body/eval_jaxpr/jit(cholesky)/cholesky | solution.py:20
  133.8 19.7 %custom-call.39 = f32[2,128,128]{1,2,0:T(8,128)S(1)} custom-call(f32[2,128,128]{2,1,0:T(8,128)S(1)} %get-tuple-element.219), custom_call_target="InvertDiagBlocksLowerTriangular" | custom-call | tf_op jit(solution)/shard_map/while/body/eval_jaxpr/jit(_cho_solve)/triangular_solve | solution.py:22
  170.3 12.3 %all_gather.47 = f32[256,256]{0,1:T(8,128)S(1)} all-gather(f32[256,64]{0,1:T(8,128)S(1)} %bitcast.554), channel_id=1, replica_groups=mesh['chain'=64,'col'=4] {'col'}, dimensions={1}, use_global_device_ids=true | all-gather | bytes 327680 | tf_op jit(solution)/shard_map/all_gather | solution.py:103
  185.6 12.7 %all_gather.48 = f32[256,256]{0,1:T(8,128)S(1)} all-gather(f32[256,64]{0,1:T(8,128)S(1)} %fusion.17), channel_id=1, replica_groups=mesh['chain'=64,'col'=4] {'col'}, dimensions={1}, use_global_device_ids=true | all-gather | bytes 327680 | tf_op jit(solution)/shard_map/all_gather | solution.py:102
  220.6 11.7 %cholesky.509 = f32[128,128]{1,0:T(8,128)S(1)} custom-call(f32[128,128]{1,0:T(8,128)S(1)} %convolution_subtract_fusion.22), custom_call_target="Cholesky" | custom-call | tf_op jit(solution)/shard_map/jit(cholesky)/cholesky | solution.py:20
  240.0 19.7 %custom-call.41 = f32[2,128,128]{1,2,0:T(8,128)S(1)} custom-call(f32[2,128,128]{2,1,0:T(8,128)S(1)} %get-tuple-element.220), custom_call_target="InvertDiagBlocksLowerTriangular" | custom-call | tf_op jit(solution)/shard_map/jit(_cho_solve)/triangular_solve | solution.py:22
  276.8 12.2 %all_gather.49 = f32[256,256]{0,1:T(8,128)S(1)} all-gather(f32[256,64]{0,1:T(8,128)S(1)} %convolution_negate_fusion.5), channel_id=1, replica_groups=mesh['chain'=64,'col'=4] {'col'}, dimensions={1}, use_global_device_ids=true | all-gather | bytes 327680 | tf_op jit(solution)/shard_map/all_gather | solution.py:103
  290.3 12.3 %all_gather.50 = f32[256,256]{0,1:T(8,128)S(1)} all-gather(f32[256,64]{0,1:T(8,128)S(1)} %subtract_subtract_fusion.5), channel_id=1, replica_groups=mesh['chain'=64,'col'=4] {'col'}, dimensions={1}, use_global_device_ids=true | all-gather | bytes 327680 | tf_op jit(solution)/shard_map/all_gather | solution.py:102
  344.9 19.7 %custom-call.43 = f32[2,128,128]{1,2,0:T(8,128)S(1)} custom-call(f32[2,128,128]{2,1,0:T(8,128)S(1)} %get-tuple-element.221), custom_call_target="InvertDiagBlocksLowerTriangular" | custom-call | tf_op jit(solution)/shard_map/jit(_cho_solve)/triangular_solve | solution.py:22
  384.7 12.3 %all_gather.51 = f32[256,256]{0,1:T(8,128)S(1)} all-gather(f32[256,64]{0,1:T(8,128)S(1)} %convolution_negate_fusion.4), channel_id=1, replica_groups=mesh['chain'=64,'col'=4] {'col'}, dimensions={1}, use_global_device_ids=true | all-gather | bytes 327680 | tf_op jit(solution)/shard_map/all_gather | solution.py:103
  398.5 12.2 %all_gather.52 = f32[256,256]{0,1:T(8,128)S(1)} all-gather(f32[256,64]{0,1:T(8,128)S(1)} %subtract_subtract_fusion.4), channel_id=1, replica_groups=mesh['chain'=64,'col'=4] {'col'}, dimensions={1}, use_global_device_ids=true | all-gather | bytes 327680 | tf_op jit(solution)/shard_map/all_gather | solution.py:102
  433.0 11.7 %cholesky.577 = f32[128,128]{1,0:T(8,128)S(1)} custom-call(f32[128,128]{1,0:T(8,128)S(1)} %convolution_subtract_fusion.20), custom_call_target="Cholesky" | custom-call | tf_op jit(solution)/shard_map/jit(cholesky)/cholesky | solution.py:20
  451.8 19.7 %custom-call.45 = f32[2,128,128]{1,2,0:T(8,128)S(1)} custom-call(f32[2,128,128]{2,1,0:T(8,128)S(1)} %get-tuple-element.222), custom_call_target="InvertDiagBlocksLowerTriangular" | custom-call | tf_op jit(solution)/shard_map/jit(_cho_solve)/triangular_solve | solution.py:22
  497.7 12.3 %all_gather.53 = f32[256,256]{0,1:T(8,128)S(1)} all-gather(f32[256,64]{0,1:T(8,128)S(1)} %convolution_negate_fusion.3), channel_id=1, replica_groups=mesh['chain'=64,'col'=4] {'col'}, dimensions={1}, use_global_device_ids=true | all-gather | bytes 327680 | tf_op jit(solution)/shard_map/all_gather | solution.py:103
  511.2 12.3 %all_gather.54 = f32[256,256]{0,1:T(8,128)S(1)} all-gather(f32[256,64]{0,1:T(8,128)S(1)} %subtract_subtract_fusion.3), channel_id=1, replica_groups=mesh['chain'=64,'col'=4] {'col'}, dimensions={1}, use_global_device_ids=true | all-gather | bytes 327680 | tf_op jit(solution)/shard_map/all_gather | solution.py:102
  545.7 11.7 %cholesky.611 = f32[128,128]{1,0:T(8,128)S(1)} custom-call(f32[128,128]{1,0:T(8,128)S(1)} %convolution_subtract_fusion.19), custom_call_target="Cholesky" | custom-call | tf_op jit(solution)/shard_map/jit(cholesky)/cholesky | solution.py:20
  565.5 19.7 %custom-call.47 = f32[2,128,128]{1,2,0:T(8,128)S(1)} custom-call(f32[2,128,128]{2,1,0:T(8,128)S(1)} %get-tuple-element.223), custom_call_target="InvertDiagBlocksLowerTriangular" | custom-call | tf_op jit(solution)/shard_map/jit(_cho_solve)/triangular_solve | solution.py:22
  606.4 12.2 %all_gather.55 = f32[256,256]{0,1:T(8,128)S(1)} all-gather(f32[256,64]{0,1:T(8,128)S(1)} %convolution_negate_fusion.2), channel_id=1, replica_groups=mesh['chain'=64,'col'=4] {'col'}, dimensions={1}, use_global_device_ids=true | all-gather | bytes 327680 | tf_op jit(solution)/shard_map/all_gather | solution.py:103
  620.1 12.2 %all_gather.56 = f32[256,256]{0,1:T(8,128)S(1)} all-gather(f32[256,64]{0,1:T(8,128)S(1)} %subtract_subtract_fusion.2), channel_id=1, replica_groups=mesh['chain'=64,'col'=4] {'col'}, dimensions={1}, use_global_device_ids=true | all-gather | bytes 327680 | tf_op jit(solution)/shard_map/all_gather | solution.py:102
  654.6 11.7 %cholesky.645 = f32[128,128]{1,0:T(8,128)S(1)} custom-call(f32[128,128]{1,0:T(8,128)S(1)} %convolution_subtract_fusion.18), custom_call_target="Cholesky" | custom-call | tf_op jit(solution)/shard_map/jit(cholesky)/cholesky | solution.py:20
  673.8 19.7 %custom-call.49 = f32[2,128,128]{1,2,0:T(8,128)S(1)} custom-call(f32[2,128,128]{2,1,0:T(8,128)S(1)} %get-tuple-element.224), custom_call_target="InvertDiagBlocksLowerTriangular" | custom-call | tf_op jit(solution)/shard_map/jit(_cho_solve)/triangular_solve | solution.py:22
  720.7 12.2 %all_gather.57 = f32[256,256]{0,1:T(8,128)S(1)} all-gather(f32[256,64]{0,1:T(8,128)S(1)} %convolution_negate_fusion.1), channel_id=1, replica_groups=mesh['chain'=64,'col'=4] {'col'}, dimensions={1}, use_global_device_ids=true | all-gather | bytes 327680 | tf_op jit(solution)/shard_map/all_gather | solution.py:103
  734.2 12.3 %all_gather.58 = f32[256,256]{0,1:T(8,128)S(1)} all-gather(f32[256,64]{0,1:T(8,128)S(1)} %subtract_subtract_fusion.1), channel_id=1, replica_groups=mesh['chain'=64,'col'=4] {'col'}, dimensions={1}, use_global_device_ids=true | all-gather | bytes 327680 | tf_op jit(solution)/shard_map/all_gather | solution.py:102
  768.7 11.7 %cholesky.679 = f32[128,128]{1,0:T(8,128)S(1)} custom-call(f32[128,128]{1,0:T(8,128)S(1)} %convolution_subtract_fusion.17), custom_call_target="Cholesky" | custom-call | tf_op jit(solution)/shard_map/jit(cholesky)/cholesky | solution.py:20
  789.2 19.7 %custom-call.51 = f32[2,128,128]{1,2,0:T(8,128)S(1)} custom-call(f32[2,128,128]{2,1,0:T(8,128)S(1)} %get-tuple-element.225), custom_call_target="InvertDiagBlocksLowerTriangular" | custom-call | tf_op jit(solution)/shard_map/jit(_cho_solve)/triangular_solve | solution.py:22
  840.2 12.3 %all_gather.59 = f32[256,256]{0,1:T(8,128)S(1)} all-gather(f32[256,64]{0,1:T(8,128)S(1)} %subtract_subtract_fusion), channel_id=1, replica_groups=mesh['chain'=64,'col'=4] {'col'}, dimensions={1}, use_global_device_ids=true | all-gather | bytes 327680 | tf_op jit(solution)/shard_map/all_gather | solution.py:118
  874.7 11.7 %cholesky.713 = f32[128,128]{1,0:T(8,128)S(1)} custom-call(f32[128,128]{1,0:T(8,128)S(1)} %convolution_subtract_fusion.16), custom_call_target="Cholesky" | custom-call | tf_op jit(solution)/shard_map/jit(cholesky)/cholesky | solution.py:119
  893.8 19.7 %custom-call.20 = f32[2,128,128]{1,2,0:T(8,128)S(1)} custom-call(f32[2,128,128]{2,1,0:T(8,128)S(1)} %get-tuple-element.175), custom_call_target="InvertDiagBlocksLowerTriangular" | custom-call | tf_op jit(solution)/shard_map/jit(_cho_solve)/triangular_solve | solution.py:119
  (472 shorter events, 493.2 us)
Async XLA Ops:
  158.3 10.2 %collective-permute-start.19 = (f32[16,256]{1,0:T(8,128)}, f32[16,256]{1,0:T(8,128)S(1)}, u32[]{:S(2)}, u32[]{:S(2)}) collective-permute-start(f32[16,256]{1,0:T(8,128)} %convolution_subtract_fusion.29), channel_id=1, source_target_pairs={{4,0},{8,4},{12,8},{16,12},{20,16},{24,20},{28,24},{32,28},{36,32}... | collective-permute-start | bytes 49160 | tf_op jit(solution)/shard_map/ppermute | solution.py:12
  161.7 20.9 %collective-permute-start = (f32[256,256]{1,0:T(8,128)}, f32[256,256]{1,0:T(8,128)S(1)}, u32[]{:S(2)}, u32[]{:S(2)}) collective-permute-start(f32[256,256]{1,0:T(8,128)} %convolution_add_fusion), channel_id=1, source_target_pairs={{4,0},{8,4},{12,8},{16,12},{20,16},{24,20},{28,24},{32,28},{36,32}... | collective-permute-start | bytes 786440 | tf_op jit(solution)/shard_map/ppermute | solution.py:12
  262.1 13.5 %collective-permute-start.21 = (f32[16,256]{1,0:T(8,128)S(1)}, f32[16,256]{1,0:T(8,128)S(1)}, u32[]{:S(2)}, u32[]{:S(2)}) collective-permute-start(f32[16,256]{1,0:T(8,128)S(1)} %fusion.228), channel_id=1, source_target_pairs={{4,0},{8,4},{12,8},{16,12},{20,16},{24,20},{28,24},{32,28},{36,32}... | collective-permute-start | bytes 49160 | tf_op jit(solution)/shard_map/ppermute | solution.py:12
  265.4 10.4 %collective-permute-start.4 = (f32[256,64]{0,1:T(8,128)S(1)}, f32[256,64]{0,1:T(8,128)S(1)}, u32[]{:S(2)}, u32[]{:S(2)}) collective-permute-start(f32[256,64]{0,1:T(8,128)S(1)} %fusion.229), channel_id=1, source_target_pairs={{4,0},{8,4},{12,8},{16,12},{20,16},{24,20},{28,24},{32,28},{36,32}... | collective-permute-start | bytes 196616 | tf_op jit(solution)/shard_map/ppermute | solution.py:12
  268.1 99.2 %collective-permute-start.20 = (f32[16,256]{1,0:T(8,128)}, f32[16,256]{1,0:T(8,128)S(1)}, u32[]{:S(2)}, u32[]{:S(2)}) collective-permute-start(f32[16,256]{1,0:T(8,128)} %fusion.247), channel_id=1, source_target_pairs={{0,4},{4,8},{8,12},{12,16},{16,20},{20,24},{24,28},{28,32},{32,36}... | collective-permute-start | bytes 49160 | tf_op jit(solution)/shard_map/ppermute | solution.py:12
  270.1 19.0 %collective-permute-start.3 = (f32[256,256]{1,0:T(8,128)S(1)}, f32[256,256]{1,0:T(8,128)S(1)}, u32[]{:S(2)}, u32[]{:S(2)}) collective-permute-start(f32[256,256]{1,0:T(8,128)S(1)} %pad_maximum_fusion.3), channel_id=1, source_target_pairs={{4,0},{8,4},{12,8},{16,12},{20,16},{24,20},{28,24},{32,28},{36,32}... | collective-permute-start | bytes 786440 | tf_op jit(solution)/shard_map/ppermute | solution.py:12
  273.7 15.8 %collective-permute-start.2 = (f32[256,64]{0,1:T(8,128)S(1)}, f32[256,64]{0,1:T(8,128)S(1)}, u32[]{:S(2)}, u32[]{:S(2)}) collective-permute-start(f32[256,64]{0,1:T(8,128)S(1)} %fusion.241), channel_id=1, source_target_pairs={{0,4},{4,8},{8,12},{12,16},{16,20},{20,24},{24,28},{28,32},{32,36}... | collective-permute-start | bytes 196616 | tf_op jit(solution)/shard_map/ppermute | solution.py:12
  367.9 16.2 %collective-permute-start.23 = (f32[16,256]{1,0:T(8,128)S(1)}, f32[16,256]{1,0:T(8,128)S(1)}, u32[]{:S(2)}, u32[]{:S(2)}) collective-permute-start(f32[16,256]{1,0:T(8,128)S(1)} %fusion.209), channel_id=1, source_target_pairs={{8,0},{12,4},{16,8},{20,12},{24,16},{28,20},{32,24},{36,28},{40,32... | collective-permute-start | bytes 49160 | tf_op jit(solution)/shard_map/ppermute | solution.py:12
  370.8 13.4 %collective-permute-start.22 = (f32[16,256]{1,0:T(8,128)S(1)}, f32[16,256]{1,0:T(8,128)S(1)}, u32[]{:S(2)}, u32[]{:S(2)}) collective-permute-start(f32[16,256]{1,0:T(8,128)S(1)} %fusion.249), channel_id=1, source_target_pairs={{0,8},{4,12},{8,16},{12,20},{16,24},{20,28},{24,32},{28,36},{32,40... | collective-permute-start | bytes 49160 | tf_op jit(solution)/shard_map/ppermute | solution.py:12
  372.5 11.9 %collective-permute-start.7 = (f32[256,64]{0,1:T(8,128)S(1)}, f32[256,64]{0,1:T(8,128)S(1)}, u32[]{:S(2)}, u32[]{:S(2)}) collective-permute-start(f32[256,64]{0,1:T(8,128)S(1)} %fusion.227), channel_id=1, source_target_pairs={{8,0},{12,4},{16,8},{20,12},{24,16},{28,20},{32,24},{36,28},{40,32... | collective-permute-start | bytes 196616 | tf_op jit(solution)/shard_map/ppermute | solution.py:12
  378.2 18.8 %collective-permute-start.6 = (f32[256,256]{1,0:T(8,128)S(1)}, f32[256,256]{1,0:T(8,128)S(1)}, u32[]{:S(2)}, u32[]{:S(2)}) collective-permute-start(f32[256,256]{1,0:T(8,128)S(1)} %pad_maximum_fusion.4), channel_id=1, source_target_pairs={{8,0},{12,4},{16,8},{20,12},{24,16},{28,20},{32,24},{36,28},{40,32... | collective-permute-start | bytes 786440 | tf_op jit(solution)/shard_map/ppermute | solution.py:12
  382.9 14.6 %collective-permute-start.5 = (f32[256,64]{0,1:T(8,128)S(1)}, f32[256,64]{0,1:T(8,128)S(1)}, u32[]{:S(2)}, u32[]{:S(2)}) collective-permute-start(f32[256,64]{0,1:T(8,128)S(1)} %fusion.242), channel_id=1, source_target_pairs={{0,8},{4,12},{8,16},{12,20},{16,24},{20,28},{24,32},{28,36},{32,40... | collective-permute-start | bytes 196616 | tf_op jit(solution)/shard_map/ppermute | solution.py:12
  474.5 22.1 %collective-permute-start.25 = (f32[16,256]{1,0:T(8,128)S(1)}, f32[16,256]{1,0:T(8,128)S(1)}, u32[]{:S(2)}, u32[]{:S(2)}) collective-permute-start(f32[16,256]{1,0:T(8,128)S(1)} %fusion.225), channel_id=1, source_target_pairs={{16,0},{20,4},{24,8},{28,12},{32,16},{36,20},{40,24},{44,28},{48,3... | collective-permute-start | bytes 49160 | tf_op jit(solution)/shard_map/ppermute | solution.py:12
  483.0 13.8 %collective-permute-start.10 = (f32[256,64]{0,1:T(8,128)S(1)}, f32[256,64]{0,1:T(8,128)S(1)}, u32[]{:S(2)}, u32[]{:S(2)}) collective-permute-start(f32[256,64]{0,1:T(8,128)S(1)} %fusion.226), channel_id=1, source_target_pairs={{16,0},{20,4},{24,8},{28,12},{32,16},{36,20},{40,24},{44,28},{48,3... | collective-permute-start | bytes 196616 | tf_op jit(solution)/shard_map/ppermute | solution.py:12
  487.9 100.0 %collective-permute-start.24 = (f32[16,256]{1,0:T(8,128)}, f32[16,256]{1,0:T(8,128)S(1)}, u32[]{:S(2)}, u32[]{:S(2)}) collective-permute-start(f32[16,256]{1,0:T(8,128)} %fusion.250), channel_id=1, source_target_pairs={{0,16},{4,20},{8,24},{12,28},{16,32},{20,36},{24,40},{28,44},{32,4... | collective-permute-start | bytes 49160 | tf_op jit(solution)/shard_map/ppermute | solution.py:12
  489.2 20.8 %collective-permute-start.9 = (f32[256,256]{1,0:T(8,128)S(1)}, f32[256,256]{1,0:T(8,128)S(1)}, u32[]{:S(2)}, u32[]{:S(2)}) collective-permute-start(f32[256,256]{1,0:T(8,128)S(1)} %pad_maximum_fusion.5), channel_id=1, source_target_pairs={{16,0},{20,4},{24,8},{28,12},{32,16},{36,20},{40,24},{44,28},{48,3... | collective-permute-start | bytes 786440 | tf_op jit(solution)/shard_map/ppermute | solution.py:12
  495.2 15.2 %collective-permute-start.8 = (f32[256,64]{0,1:T(8,128)S(1)}, f32[256,64]{0,1:T(8,128)S(1)}, u32[]{:S(2)}, u32[]{:S(2)}) collective-permute-start(f32[256,64]{0,1:T(8,128)S(1)} %fusion.243), channel_id=1, source_target_pairs={{0,16},{4,20},{8,24},{12,28},{16,32},{20,36},{24,40},{28,44},{32,4... | collective-permute-start | bytes 196616 | tf_op jit(solution)/shard_map/ppermute | solution.py:12
  588.5 17.3 %collective-permute-start.27 = (f32[16,256]{1,0:T(8,128)S(1)}, f32[16,256]{1,0:T(8,128)S(1)}, u32[]{:S(2)}, u32[]{:S(2)}) collective-permute-start(f32[16,256]{1,0:T(8,128)S(1)} %fusion.210), channel_id=1, source_target_pairs={{32,0},{36,4},{40,8},{44,12},{48,16},{52,20},{56,24},{60,28},{64,3... | collective-permute-start | bytes 49160 | tf_op jit(solution)/shard_map/ppermute | solution.py:12
  594.7 11.2 %collective-permute-start.26 = (f32[16,256]{1,0:T(8,128)S(1)}, f32[16,256]{1,0:T(8,128)S(1)}, u32[]{:S(2)}, u32[]{:S(2)}) collective-permute-start(f32[16,256]{1,0:T(8,128)S(1)} %fusion.252), channel_id=1, source_target_pairs={{0,32},{4,36},{8,40},{12,44},{16,48},{20,52},{24,56},{28,60},{32,6... | collective-permute-start | bytes 49160 | tf_op jit(solution)/shard_map/ppermute | solution.py:12
  596.4 9.7 %collective-permute-start.13 = (f32[256,64]{0,1:T(8,128)S(1)}, f32[256,64]{0,1:T(8,128)S(1)}, u32[]{:S(2)}, u32[]{:S(2)}) collective-permute-start(f32[256,64]{0,1:T(8,128)S(1)} %fusion.224), channel_id=1, source_target_pairs={{32,0},{36,4},{40,8},{44,12},{48,16},{52,20},{56,24},{60,28},{64,3... | collective-permute-start | bytes 196616 | tf_op jit(solution)/shard_map/ppermute | solution.py:12
  601.0 17.7 %collective-permute-start.12 = (f32[256,256]{1,0:T(8,128)S(1)}, f32[256,256]{1,0:T(8,128)S(1)}, u32[]{:S(2)}, u32[]{:S(2)}) collective-permute-start(f32[256,256]{1,0:T(8,128)S(1)} %pad_maximum_fusion.6), channel_id=1, source_target_pairs={{32,0},{36,4},{40,8},{44,12},{48,16},{52,20},{56,24},{60,28},{64,3... | collective-permute-start | bytes 786440 | tf_op jit(solution)/shard_map/ppermute | solution.py:12
  604.5 14.6 %collective-permute-start.11 = (f32[256,64]{0,1:T(8,128)S(1)}, f32[256,64]{0,1:T(8,128)S(1)}, u32[]{:S(2)}, u32[]{:S(2)}) collective-permute-start(f32[256,64]{0,1:T(8,128)S(1)} %fusion.244), channel_id=1, source_target_pairs={{0,32},{4,36},{8,40},{12,44},{16,48},{20,52},{24,56},{28,60},{32,6... | collective-permute-start | bytes 196616 | tf_op jit(solution)/shard_map/ppermute | solution.py:12
  696.5 23.1 %collective-permute-start.29 = (f32[16,256]{1,0:T(8,128)S(1)}, f32[16,256]{1,0:T(8,128)S(1)}, u32[]{:S(2)}, u32[]{:S(2)}) collective-permute-start(f32[16,256]{1,0:T(8,128)S(1)} %fusion.222), channel_id=1, source_target_pairs={{64,0},{68,4},{72,8},{76,12},{80,16},{84,20},{88,24},{92,28},{96,3... | collective-permute-start | bytes 49160 | tf_op jit(solution)/shard_map/ppermute | solution.py:12
  706.9 12.9 %collective-permute-start.16 = (f32[256,64]{0,1:T(8,128)S(1)}, f32[256,64]{0,1:T(8,128)S(1)}, u32[]{:S(2)}, u32[]{:S(2)}) collective-permute-start(f32[256,64]{0,1:T(8,128)S(1)} %fusion.223), channel_id=1, source_target_pairs={{64,0},{68,4},{72,8},{76,12},{80,16},{84,20},{88,24},{92,28},{96,3... | collective-permute-start | bytes 196616 | tf_op jit(solution)/shard_map/ppermute | solution.py:12
  711.5 100.1 %collective-permute-start.28 = (f32[16,256]{1,0:T(8,128)}, f32[16,256]{1,0:T(8,128)S(1)}, u32[]{:S(2)}, u32[]{:S(2)}) collective-permute-start(f32[16,256]{1,0:T(8,128)} %fusion.253), channel_id=1, source_target_pairs={{0,64},{4,68},{8,72},{12,76},{16,80},{20,84},{24,88},{28,92},{32,9... | collective-permute-start | bytes 49160 | tf_op jit(solution)/shard_map/ppermute | solution.py:12
  712.8 20.2 %collective-permute-start.15 = (f32[256,256]{1,0:T(8,128)S(1)}, f32[256,256]{1,0:T(8,128)S(1)}, u32[]{:S(2)}, u32[]{:S(2)}) collective-permute-start(f32[256,256]{1,0:T(8,128)S(1)} %pad_maximum_fusion.7), channel_id=1, source_target_pairs={{64,0},{68,4},{72,8},{76,12},{80,16},{84,20},{88,24},{92,28},{96,3... | collective-permute-start | bytes 786440 | tf_op jit(solution)/shard_map/ppermute | solution.py:12
  718.3 15.2 %collective-permute-start.14 = (f32[256,64]{0,1:T(8,128)S(1)}, f32[256,64]{0,1:T(8,128)S(1)}, u32[]{:S(2)}, u32[]{:S(2)}) collective-permute-start(f32[256,64]{0,1:T(8,128)S(1)} %fusion.245), channel_id=1, source_target_pairs={{0,64},{4,68},{8,72},{12,76},{16,80},{20,84},{24,88},{28,92},{32,9... | collective-permute-start | bytes 196616 | tf_op jit(solution)/shard_map/ppermute | solution.py:12
  811.9 19.1 %collective-permute-start.31 = (f32[16,256]{1,0:T(8,128)S(1)}, f32[16,256]{1,0:T(8,128)S(1)}, u32[]{:S(2)}, u32[]{:S(2)}) collective-permute-start(f32[16,256]{1,0:T(8,128)S(1)} %fusion.211), channel_id=1, source_target_pairs={{128,0},{132,4},{136,8},{140,12},{144,16},{148,20},{152,24},{156,2... | collective-permute-start | bytes 49160 | tf_op jit(solution)/shard_map/ppermute | solution.py:12
  819.5 11.5 %collective-permute-start.30 = (f32[16,256]{1,0:T(8,128)S(1)}, f32[16,256]{1,0:T(8,128)S(1)}, u32[]{:S(2)}, u32[]{:S(2)}) collective-permute-start(f32[16,256]{1,0:T(8,128)S(1)} %fusion.255), channel_id=1, source_target_pairs={{0,128},{4,132},{8,136},{12,140},{16,144},{20,148},{24,152},{28,15... | collective-permute-start | bytes 49160 | tf_op jit(solution)/shard_map/ppermute | solution.py:12
  820.8 12.3 %collective-permute-start.18 = (f32[256,256]{1,0:T(8,128)S(1)}, f32[256,256]{1,0:T(8,128)S(1)}, u32[]{:S(2)}, u32[]{:S(2)}) collective-permute-start(f32[256,256]{1,0:T(8,128)S(1)} %pad_maximum_fusion.8), channel_id=1, source_target_pairs={{128,0},{132,4},{136,8},{140,12},{144,16},{148,20},{152,24},{156,2... | collective-permute-start | bytes 786440 | tf_op jit(solution)/shard_map/ppermute | solution.py:12
  829.7 10.1 %collective-permute-start.17 = (f32[256,64]{0,1:T(8,128)S(1)}, f32[256,64]{0,1:T(8,128)S(1)}, u32[]{:S(2)}, u32[]{:S(2)}) collective-permute-start(f32[256,64]{0,1:T(8,128)S(1)} %fusion.246), channel_id=1, source_target_pairs={{0,128},{4,132},{8,136},{12,140},{16,144},{20,148},{24,152},{28,15... | collective-permute-start | bytes 196616 | tf_op jit(solution)/shard_map/ppermute | solution.py:12
  915.0 5.1 collective-permute-start.32
  (33 other events, 118.1 us)
where the time goes:
time: 934 us; the launch traced here: 924 us
  other arithmetic  490 us (52%)
  blocking collectives  187 us (20%)
  starting transfers between devices  114 us (12%)
  local copies, waits for them, and re-layouts  56.2 us (6%)
  matrix products  47.9 us (5%)
  between operations  13.9 us (1%)
  waiting for transfers between devices  12 us (1%)
    another operation x55, other arithmetic, invert(): lower_factor = jnp.linalg.cholesky(matrix)  276 us
    another operation x23, other arithmetic, invert(): return jax.scipy.linalg.cho_solve((lower_factor, True), identity)  158 us
    ppermute x33, starting transfers between devices, passed_along(): return lax.ppermute(shard, axis, pairs)  114 us
    all_gather x6, blocking collectives, per_device(): lax.all_gather(b_part, 'col', axis=1, tiled=True)  74 us
    all_gather x6, blocking collectives, per_device(): lax.all_gather(c_part, 'col', axis=1, tiled=True)  73.5 us
    another operation x58, local copies, waits for them, and re-layouts, invert(): return jax.scipy.linalg.cho_solve((lower_factor, True), identity)  35.5 us
    another operation x7, other arithmetic, per_device(): jnp.linalg.cholesky(b_final)  34.6 us
    dot_general x71, matrix products, matmul(): return jnp.dot(first_factor, second_factor, precision=finest)  28.7 us
  transfers between devices with their start and end apart: 33, of which 4 were waited for; matrix products, arithmetic and copies ran while one was open for 22% of the time, Pallas kernels for 0%

commit v1 on v0

--- a/solution.py
+++ b/solution.py
@@ -99,7 +99,9 @@
     for level_index in range(levels):
         distance = 1 << level_index
         b_full, c_full = (
-            lax.all_gather(b_part, "col", axis=1, tiled=True),
+            jnp.concatenate(
+                lax.all_to_all(jnp.stack([b_part] * lax.axis_size("col")), "col", 0, 0), axis=1
+            ),
             lax.all_gather(c_part, "col", axis=1, tiled=True),
         )
         inverse = invert(b_full)

time: 934 us -> 906 us (0.970)
  blocking collectives: 187 us -> 114 us
  waiting for transfers between devices: 12 us -> 35.9 us
  starting transfers between devices: 114 us -> 124 us
    all_gather x6 -> x0, blocking collectives: 74 us -> none  [per_device(): lax.all_gather(b_part, 'col', axis=1, tiled=True)]
    all_to_all x0 -> x6, starting transfers between devices: none -> 28.1 us  [per_device(): lax.all_to_all(jnp.stack([b_part] * lax.axis_size('col')), 'col', 0, 0)]
    ppermute x33, waiting for transfers between devices: 12 us -> 35.9 us  [passed_along(): return lax.ppermute(shard, axis, pairs)]
    ppermute x33, starting transfers between devices: 114 us -> 95.9 us  [passed_along(): return lax.ppermute(shard, axis, pairs)]
  transfers between devices with their start and end apart: 33 -> 39, of which waited for: 4 -> 9; matrix products, arithmetic and copies ran while one was open for 22% -> 24% of each run, Pallas kernels for 0% -> 0%
where the time goes in v1:
time: 906 us; the launch traced here: 890 us
  other arithmetic  491 us (54%)
  starting transfers between devices  124 us (14%)
  blocking collectives  114 us (13%)
  local copies, waits for them, and re-layouts  55.2 us (6%)
  matrix products  53.4 us (6%)
  waiting for transfers between devices  35.9 us (4%)
  between operations  14.4 us (2%)
    another operation x55, other arithmetic, invert(): lower_factor = jnp.linalg.cholesky(matrix)  277 us
    another operation x23, other arithmetic, invert(): return jax.scipy.linalg.cho_solve((lower_factor, True), identity)  158 us
    ppermute x33, starting transfers between devices, passed_along(): return lax.ppermute(shard, axis, pairs)  95.9 us
    all_gather x6, blocking collectives, per_device(): lax.all_gather(c_part, 'col', axis=1, tiled=True)  74.1 us
    another operation x58, local copies, waits for them, and re-layouts, invert(): return jax.scipy.linalg.cho_solve((lower_factor, True), identity)  36.8 us
    ppermute x33, waiting for transfers between devices, passed_along(): return lax.ppermute(shard, axis, pairs)  35.9 us
    another operation x7, other arithmetic, per_device(): jnp.linalg.cholesky(b_final)  34.6 us
    dot_general x71, matrix products, matmul(): return jnp.dot(first_factor, second_factor, precision=finest)  34.2 us
  transfers between devices with their start and end apart: 39, of which 9 were waited for; matrix products, arithmetic and copies ran while one was open for 24% of the time, Pallas kernels for 0%

profile of v1, /device:TPU:250, one launch (start us, length us, event | category | flops | bytes accessed | tf_op | source)
XLA Modules:
  0.0 889.8 jit_solution(3715239526884997599)
XLA Ops:
  1.0 13.5 %all_gather.27 = f32[2,256,256]{2,0,1:T(2,128)S(1)} all-gather(f32[2,64,256]{2,0,1:T(2,128)S(1)} %copy.26), channel_id=1, replica_groups=mesh['chain'=64,'col'=4] {'col'}, dimensions={1}, use_global_device_ids=true | all-gather | bytes 655360 | tf_op jit(solution)/shard_map/all_gather | solution.py:53
  15.1 11.7 %cholesky.424 = f32[128,128]{1,0:T(8,128)S(1)} custom-call(f32[128,128]{1,0:T(8,128)S(1)} %cholesky.726), custom_call_target="Cholesky" | custom-call | tf_op jit(solution)/shard_map/jit(cholesky)/cholesky | solution.py:20
  37.2 11.7 %cholesky.441 = f32[128,128]{1,0:T(8,128)S(1)} custom-call(f32[128,128]{1,0:T(8,128)S(1)} %convolution_subtract_fusion.24), custom_call_target="Cholesky" | custom-call | tf_op jit(solution)/shard_map/jit(cholesky)/cholesky | solution.py:20
  55.1 19.7 %custom-call.37 = f32[2,128,128]{1,2,0:T(8,128)S(1)} custom-call(f32[2,128,128]{2,1,0:T(8,128)S(1)} %get-tuple-element.218), custom_call_target="InvertDiagBlocksLowerTriangular" | custom-call | tf_op jit(solution)/shard_map/jit(_cho_solve)/triangular_solve | solution.py:22
  77.2 14.0 %all_gather.28 = f32[3,256,256]{2,1,0:T(8,128)S(1)} all-gather(f32[3,64,256]{2,1,0:T(8,128)S(1)} %copy-done.13), channel_id=1, replica_groups=mesh['chain'=64,'col'=4] {'col'}, dimensions={1}, use_global_device_ids=true | all-gather | bytes 983040 | tf_op jit(solution)/shard_map/all_gather | solution.py:54
  93.3 11.7 %cholesky.458 = f32[128,128]{1,0:T(8,128)S(1)} custom-call(f32[128,128]{1,0:T(8,128)S(1)} %cholesky.729), custom_call_target="Cholesky" | custom-call | tf_op jit(solution)/shard_map/while/body/eval_jaxpr/jit(cholesky)/cholesky | solution.py:20
  115.4 11.7 %cholesky.475 = f32[128,128]{1,0:T(8,128)S(1)} custom-call(f32[128,128]{1,0:T(8,128)S(1)} %convolution_subtract_fusion.23), custom_call_target="Cholesky" | custom-call | tf_op jit(solution)/shard_map/while/body/eval_jaxpr/jit(cholesky)/cholesky | solution.py:20
  134.1 19.7 %custom-call.39 = f32[2,128,128]{1,2,0:T(8,128)S(1)} custom-call(f32[2,128,128]{2,1,0:T(8,128)S(1)} %get-tuple-element.219), custom_call_target="InvertDiagBlocksLowerTriangular" | custom-call | tf_op jit(solution)/shard_map/while/body/eval_jaxpr/jit(_cho_solve)/triangular_solve | solution.py:22
  175.5 12.8 %all_gather.29 = f32[256,256]{0,1:T(8,128)S(1)} all-gather(f32[256,64]{0,1:T(8,128)S(1)} %bitcast.584), channel_id=1, replica_groups=mesh['chain'=64,'col'=4] {'col'}, dimensions={1}, use_global_device_ids=true | all-gather | bytes 327680 | tf_op jit(solution)/shard_map/all_gather | solution.py:105
  188.5 11.7 %cholesky.492 = f32[128,128]{1,0:T(8,128)S(1)} custom-call(f32[128,128]{1,0:T(8,128)S(1)} %cholesky.732), custom_call_target="Cholesky" | custom-call | tf_op jit(solution)/shard_map/jit(cholesky)/cholesky | solution.py:20
  210.5 11.7 %cholesky.509 = f32[128,128]{1,0:T(8,128)S(1)} custom-call(f32[128,128]{1,0:T(8,128)S(1)} %convolution_subtract_fusion.22), custom_call_target="Cholesky" | custom-call | tf_op jit(solution)/shard_map/jit(cholesky)/cholesky | solution.py:20
  230.1 19.7 %custom-call.41 = f32[2,128,128]{1,2,0:T(8,128)S(1)} custom-call(f32[2,128,128]{2,1,0:T(8,128)S(1)} %get-tuple-element.220), custom_call_target="InvertDiagBlocksLowerTriangular" | custom-call | tf_op jit(solution)/shard_map/jit(_cho_solve)/triangular_solve | solution.py:22
  277.6 12.3 %all_gather.30 = f32[256,256]{0,1:T(8,128)S(1)} all-gather(f32[256,64]{0,1:T(8,128)S(1)} %convolution_negate_fusion.5), channel_id=1, replica_groups=mesh['chain'=64,'col'=4] {'col'}, dimensions={1}, use_global_device_ids=true | all-gather | bytes 327680 | tf_op jit(solution)/shard_map/all_gather | solution.py:105
  290.0 11.7 %cholesky.526 = f32[128,128]{1,0:T(8,128)S(1)} custom-call(f32[128,128]{1,0:T(8,128)S(1)} %cholesky.735), custom_call_target="Cholesky" | custom-call | tf_op jit(solution)/shard_map/jit(cholesky)/cholesky | solution.py:20
  312.1 11.7 %cholesky.543 = f32[128,128]{1,0:T(8,128)S(1)} custom-call(f32[128,128]{1,0:T(8,128)S(1)} %convolution_subtract_fusion.21), custom_call_target="Cholesky" | custom-call | tf_op jit(solution)/shard_map/jit(cholesky)/cholesky | solution.py:20
  332.6 19.7 %custom-call.43 = f32[2,128,128]{1,2,0:T(8,128)S(1)} custom-call(f32[2,128,128]{2,1,0:T(8,128)S(1)} %get-tuple-element.221), custom_call_target="InvertDiagBlocksLowerTriangular" | custom-call | tf_op jit(solution)/shard_map/jit(_cho_solve)/triangular_solve | solution.py:22
  381.4 12.3 %all_gather.31 = f32[256,256]{0,1:T(8,128)S(1)} all-gather(f32[256,64]{0,1:T(8,128)S(1)} %convolution_negate_fusion.4), channel_id=1, replica_groups=mesh['chain'=64,'col'=4] {'col'}, dimensions={1}, use_global_device_ids=true | all-gather | bytes 327680 | tf_op jit(solution)/shard_map/all_gather | solution.py:105
  393.8 11.7 %cholesky.560 = f32[128,128]{1,0:T(8,128)S(1)} custom-call(f32[128,128]{1,0:T(8,128)S(1)} %cholesky.738), custom_call_target="Cholesky" | custom-call | tf_op jit(solution)/shard_map/jit(cholesky)/cholesky | solution.py:20
  415.9 11.7 %cholesky.577 = f32[128,128]{1,0:T(8,128)S(1)} custom-call(f32[128,128]{1,0:T(8,128)S(1)} %convolution_subtract_fusion.20), custom_call_target="Cholesky" | custom-call | tf_op jit(solution)/shard_map/jit(cholesky)/cholesky | solution.py:20
  435.2 19.7 %custom-call.45 = f32[2,128,128]{1,2,0:T(8,128)S(1)} custom-call(f32[2,128,128]{2,1,0:T(8,128)S(1)} %get-tuple-element.222), custom_call_target="InvertDiagBlocksLowerTriangular" | custom-call | tf_op jit(solution)/shard_map/jit(_cho_solve)/triangular_solve | solution.py:22
  491.3 12.3 %all_gather.32 = f32[256,256]{0,1:T(8,128)S(1)} all-gather(f32[256,64]{0,1:T(8,128)S(1)} %convolution_negate_fusion.3), channel_id=1, replica_groups=mesh['chain'=64,'col'=4] {'col'}, dimensions={1}, use_global_device_ids=true | all-gather | bytes 327680 | tf_op jit(solution)/shard_map/all_gather | solution.py:105
  525.8 11.7 %cholesky.611 = f32[128,128]{1,0:T(8,128)S(1)} custom-call(f32[128,128]{1,0:T(8,128)S(1)} %convolution_subtract_fusion.19), custom_call_target="Cholesky" | custom-call | tf_op jit(solution)/shard_map/jit(cholesky)/cholesky | solution.py:20
  546.4 19.7 %custom-call.47 = f32[2,128,128]{1,2,0:T(8,128)S(1)} custom-call(f32[2,128,128]{2,1,0:T(8,128)S(1)} %get-tuple-element.223), custom_call_target="InvertDiagBlocksLowerTriangular" | custom-call | tf_op jit(solution)/shard_map/jit(_cho_solve)/triangular_solve | solution.py:22
  597.5 12.3 %all_gather.33 = f32[256,256]{0,1:T(8,128)S(1)} all-gather(f32[256,64]{0,1:T(8,128)S(1)} %convolution_negate_fusion.2), channel_id=1, replica_groups=mesh['chain'=64,'col'=4] {'col'}, dimensions={1}, use_global_device_ids=true | all-gather | bytes 327680 | tf_op jit(solution)/shard_map/all_gather | solution.py:105
  632.0 11.7 %cholesky.645 = f32[128,128]{1,0:T(8,128)S(1)} custom-call(f32[128,128]{1,0:T(8,128)S(1)} %convolution_subtract_fusion.18), custom_call_target="Cholesky" | custom-call | tf_op jit(solution)/shard_map/jit(cholesky)/cholesky | solution.py:20
  651.3 19.7 %custom-call.49 = f32[2,128,128]{1,2,0:T(8,128)S(1)} custom-call(f32[2,128,128]{2,1,0:T(8,128)S(1)} %get-tuple-element.224), custom_call_target="InvertDiagBlocksLowerTriangular" | custom-call | tf_op jit(solution)/shard_map/jit(_cho_solve)/triangular_solve | solution.py:22
  702.0 12.3 %all_gather.34 = f32[256,256]{0,1:T(8,128)S(1)} all-gather(f32[256,64]{0,1:T(8,128)S(1)} %convolution_negate_fusion.1), channel_id=1, replica_groups=mesh['chain'=64,'col'=4] {'col'}, dimensions={1}, use_global_device_ids=true | all-gather | bytes 327680 | tf_op jit(solution)/shard_map/all_gather | solution.py:105
  736.5 11.7 %cholesky.679 = f32[128,128]{1,0:T(8,128)S(1)} custom-call(f32[128,128]{1,0:T(8,128)S(1)} %convolution_subtract_fusion.17), custom_call_target="Cholesky" | custom-call | tf_op jit(solution)/shard_map/jit(cholesky)/cholesky | solution.py:20
  756.9 19.7 %custom-call.51 = f32[2,128,128]{1,2,0:T(8,128)S(1)} custom-call(f32[2,128,128]{2,1,0:T(8,128)S(1)} %get-tuple-element.225), custom_call_target="InvertDiagBlocksLowerTriangular" | custom-call | tf_op jit(solution)/shard_map/jit(_cho_solve)/triangular_solve | solution.py:22
  806.3 12.3 %all_gather.35 = f32[256,256]{0,1:T(8,128)S(1)} all-gather(f32[256,64]{0,1:T(8,128)S(1)} %subtract_subtract_fusion), channel_id=1, replica_groups=mesh['chain'=64,'col'=4] {'col'}, dimensions={1}, use_global_device_ids=true | all-gather | bytes 327680 | tf_op jit(solution)/shard_map/all_gather | solution.py:120
  840.8 11.7 %cholesky.713 = f32[128,128]{1,0:T(8,128)S(1)} custom-call(f32[128,128]{1,0:T(8,128)S(1)} %convolution_subtract_fusion.16), custom_call_target="Cholesky" | custom-call | tf_op jit(solution)/shard_map/jit(cholesky)/cholesky | solution.py:121
  859.8 19.7 %custom-call.20 = f32[2,128,128]{1,2,0:T(8,128)S(1)} custom-call(f32[2,128,128]{2,1,0:T(8,128)S(1)} %get-tuple-element.175), custom_call_target="InvertDiagBlocksLowerTriangular" | custom-call | tf_op jit(solution)/shard_map/jit(_cho_solve)/triangular_solve | solution.py:121
  (472 shorter events, 463.2 us)
Async XLA Ops:
  157.9 9.5 %collective-permute-start.19 = (f32[16,256]{1,0:T(8,128)S(1)}, f32[16,256]{1,0:T(8,128)S(1)}, u32[]{:S(2)}, u32[]{:S(2)}) collective-permute-start(f32[16,256]{1,0:T(8,128)S(1)} %convolution_subtract_fusion.29), channel_id=1, source_target_pairs={{4,0},{8,4},{12,8},{16,12},{20,16},{24,20},{28,24},{32,28},{36,32}... | collective-permute-start | bytes 49160 | tf_op jit(solution)/shard_map/ppermute | solution.py:12
  165.0 10.2 %collective-permute-start.1 = (f32[256,64]{1,0:T(8,128)S(1)}, f32[256,64]{1,0:T(8,128)S(1)}, u32[]{:S(2)}, u32[]{:S(2)}) collective-permute-start(f32[256,64]{1,0:T(8,128)S(1)} %convolution_negate_fusion), channel_id=1, source_target_pairs={{4,0},{8,4},{12,8},{16,12},{20,16},{24,20},{28,24},{32,28},{36,32}... | collective-permute-start | bytes 196616 | tf_op jit(solution)/shard_map/ppermute | solution.py:12
  170.6 17.6 %all-to-all-start = ((f32[4,256,64]{1,2,0:T(8,128)}), f32[4,256,64]{1,2,0:T(8,128)S(1)}, u32[]{:S(2)}, u32[]{:S(2)}) async-start(f32[4,256,64]{1,2,0:T(8,128)} %stack.12), calls=%async_computation | async-start | bytes 524288 | tf_op jit(solution)/shard_map/all_to_all | solution.py:103
  252.9 13.5 %collective-permute-start.21 = (f32[16,256]{1,0:T(8,128)S(1)}, f32[16,256]{1,0:T(8,128)S(1)}, u32[]{:S(2)}, u32[]{:S(2)}) collective-permute-start(f32[16,256]{1,0:T(8,128)S(1)} %fusion.228), channel_id=1, source_target_pairs={{4,0},{8,4},{12,8},{16,12},{20,16},{24,20},{28,24},{32,28},{36,32}... | collective-permute-start | bytes 49160 | tf_op jit(solution)/shard_map/ppermute | solution.py:12
  254.9 11.8 %collective-permute-start.3 = (f32[256,256]{1,0:T(8,128)S(1)}, f32[256,256]{1,0:T(8,128)S(1)}, u32[]{:S(2)}, u32[]{:S(2)}) collective-permute-start(f32[256,256]{1,0:T(8,128)S(1)} %pad_maximum_fusion.3), channel_id=1, source_target_pairs={{4,0},{8,4},{12,8},{16,12},{20,16},{24,20},{28,24},{32,28},{36,32}... | collective-permute-start | bytes 786440 | tf_op jit(solution)/shard_map/ppermute | solution.py:12
  259.5 16.9 %collective-permute-start.4 = (f32[256,64]{0,1:T(8,128)}, f32[256,64]{0,1:T(8,128)}, u32[]{:S(2)}, u32[]{:S(2)}) collective-permute-start(f32[256,64]{0,1:T(8,128)} %fusion.229), channel_id=1, source_target_pairs={{4,0},{8,4},{12,8},{16,12},{20,16},{24,20},{28,24},{32,28},{36,32}... | collective-permute-start | bytes 196616 | tf_op jit(solution)/shard_map/ppermute | solution.py:12
  261.4 93.6 %collective-permute-start.20 = (f32[16,256]{1,0:T(8,128)}, f32[16,256]{1,0:T(8,128)S(1)}, u32[]{:S(2)}, u32[]{:S(2)}) collective-permute-start(f32[16,256]{1,0:T(8,128)} %fusion.247), channel_id=1, source_target_pairs={{0,4},{4,8},{8,12},{12,16},{16,20},{20,24},{24,28},{28,32},{32,36}... | collective-permute-start | bytes 49160 | tf_op jit(solution)/shard_map/ppermute | solution.py:12
  271.1 18.7 %all-to-all-start.1 = ((f32[4,256,64]{1,2,0:T(8,128)}), f32[4,256,64]{1,2,0:T(8,128)S(1)}, u32[]{:S(2)}, u32[]{:S(2)}) async-start(f32[4,256,64]{1,2,0:T(8,128)} %stack.13), calls=%async_computation.1 | async-start | bytes 524288 | tf_op jit(solution)/shard_map/all_to_all | solution.py:103
  355.7 15.0 %collective-permute-start.23 = (f32[16,256]{1,0:T(8,128)S(1)}, f32[16,256]{1,0:T(8,128)S(1)}, u32[]{:S(2)}, u32[]{:S(2)}) collective-permute-start(f32[16,256]{1,0:T(8,128)S(1)} %fusion.209), channel_id=1, source_target_pairs={{8,0},{12,4},{16,8},{20,12},{24,16},{28,20},{32,24},{36,28},{40,32... | collective-permute-start | bytes 49160 | tf_op jit(solution)/shard_map/ppermute | solution.py:12
  358.4 12.2 %collective-permute-start.22 = (f32[16,256]{1,0:T(8,128)S(1)}, f32[16,256]{1,0:T(8,128)S(1)}, u32[]{:S(2)}, u32[]{:S(2)}) collective-permute-start(f32[16,256]{1,0:T(8,128)S(1)} %fusion.249), channel_id=1, source_target_pairs={{0,8},{4,12},{8,16},{12,20},{16,24},{20,28},{24,32},{28,36},{32,40... | collective-permute-start | bytes 49160 | tf_op jit(solution)/shard_map/ppermute | solution.py:12
  359.7 11.2 %collective-permute-start.6 = (f32[256,256]{1,0:T(8,128)S(1)}, f32[256,256]{1,0:T(8,128)S(1)}, u32[]{:S(2)}, u32[]{:S(2)}) collective-permute-start(f32[256,256]{1,0:T(8,128)S(1)} %pad_maximum_fusion.4), channel_id=1, source_target_pairs={{8,0},{12,4},{16,8},{20,12},{24,16},{28,20},{32,24},{36,28},{40,32... | collective-permute-start | bytes 786440 | tf_op jit(solution)/shard_map/ppermute | solution.py:12
  364.7 16.4 %collective-permute-start.7 = (f32[256,64]{0,1:T(8,128)S(1)}, f32[256,64]{0,1:T(8,128)S(1)}, u32[]{:S(2)}, u32[]{:S(2)}) collective-permute-start(f32[256,64]{0,1:T(8,128)S(1)} %fusion.227), channel_id=1, source_target_pairs={{8,0},{12,4},{16,8},{20,12},{24,16},{28,20},{32,24},{36,28},{40,32... | collective-permute-start | bytes 196616 | tf_op jit(solution)/shard_map/ppermute | solution.py:12
  376.6 17.0 %all-to-all-start.2 = ((f32[4,256,64]{1,2,0:T(8,128)}), f32[4,256,64]{1,2,0:T(8,128)S(1)}, u32[]{:S(2)}, u32[]{:S(2)}) async-start(f32[4,256,64]{1,2,0:T(8,128)} %stack.14), calls=%async_computation.2 | async-start | bytes 524288 | tf_op jit(solution)/shard_map/all_to_all | solution.py:103
  458.0 19.3 %collective-permute-start.25 = (f32[16,256]{1,0:T(8,128)S(1)}, f32[16,256]{1,0:T(8,128)S(1)}, u32[]{:S(2)}, u32[]{:S(2)}) collective-permute-start(f32[16,256]{1,0:T(8,128)S(1)} %fusion.225), channel_id=1, source_target_pairs={{16,0},{20,4},{24,8},{28,12},{32,16},{36,20},{40,24},{44,28},{48,3... | collective-permute-start | bytes 49160 | tf_op jit(solution)/shard_map/ppermute | solution.py:12
  464.1 13.4 %collective-permute-start.9 = (f32[256,256]{1,0:T(8,128)S(1)}, f32[256,256]{1,0:T(8,128)S(1)}, u32[]{:S(2)}, u32[]{:S(2)}) collective-permute-start(f32[256,256]{1,0:T(8,128)S(1)} %pad_maximum_fusion.5), channel_id=1, source_target_pairs={{16,0},{20,4},{24,8},{28,12},{32,16},{36,20},{40,24},{44,28},{48,3... | collective-permute-start | bytes 786440 | tf_op jit(solution)/shard_map/ppermute | solution.py:12
  468.8 21.3 %collective-permute-start.10 = (f32[256,64]{0,1:T(8,128)}, f32[256,64]{0,1:T(8,128)}, u32[]{:S(2)}, u32[]{:S(2)}) collective-permute-start(f32[256,64]{0,1:T(8,128)} %fusion.226), channel_id=1, source_target_pairs={{16,0},{20,4},{24,8},{28,12},{32,16},{36,20},{40,24},{44,28},{48,3... | collective-permute-start | bytes 196616 | tf_op jit(solution)/shard_map/ppermute | solution.py:12
  474.7 94.1 %collective-permute-start.24 = (f32[16,256]{1,0:T(8,128)}, f32[16,256]{1,0:T(8,128)S(1)}, u32[]{:S(2)}, u32[]{:S(2)}) collective-permute-start(f32[16,256]{1,0:T(8,128)} %fusion.250), channel_id=1, source_target_pairs={{0,16},{4,20},{8,24},{12,28},{16,32},{20,36},{24,40},{28,44},{32,4... | collective-permute-start | bytes 49160 | tf_op jit(solution)/shard_map/ppermute | solution.py:12
  485.4 18.2 %all-to-all-start.3 = ((f32[4,256,64]{1,2,0:T(8,128)}), f32[4,256,64]{1,2,0:T(8,128)S(1)}, u32[]{:S(2)}, u32[]{:S(2)}) async-start(f32[4,256,64]{1,2,0:T(8,128)} %stack.15), calls=%async_computation.3 | async-start | bytes 524288 | tf_op jit(solution)/shard_map/all_to_all | solution.py:103
  569.4 17.3 %collective-permute-start.27 = (f32[16,256]{1,0:T(8,128)S(1)}, f32[16,256]{1,0:T(8,128)S(1)}, u32[]{:S(2)}, u32[]{:S(2)}) collective-permute-start(f32[16,256]{1,0:T(8,128)S(1)} %fusion.210), channel_id=1, source_target_pairs={{32,0},{36,4},{40,8},{44,12},{48,16},{52,20},{56,24},{60,28},{64,3... | collective-permute-start | bytes 49160 | tf_op jit(solution)/shard_map/ppermute | solution.py:12
  573.0 13.7 %collective-permute-start.26 = (f32[16,256]{1,0:T(8,128)S(1)}, f32[16,256]{1,0:T(8,128)S(1)}, u32[]{:S(2)}, u32[]{:S(2)}) collective-permute-start(f32[16,256]{1,0:T(8,128)S(1)} %fusion.252), channel_id=1, source_target_pairs={{0,32},{4,36},{8,40},{12,44},{16,48},{20,52},{24,56},{28,60},{32,6... | collective-permute-start | bytes 49160 | tf_op jit(solution)/shard_map/ppermute | solution.py:12
  574.3 12.6 %collective-permute-start.12 = (f32[256,256]{1,0:T(8,128)S(1)}, f32[256,256]{1,0:T(8,128)S(1)}, u32[]{:S(2)}, u32[]{:S(2)}) collective-permute-start(f32[256,256]{1,0:T(8,128)S(1)} %pad_maximum_fusion.6), channel_id=1, source_target_pairs={{32,0},{36,4},{40,8},{44,12},{48,16},{52,20},{56,24},{60,28},{64,3... | collective-permute-start | bytes 786440 | tf_op jit(solution)/shard_map/ppermute | solution.py:12
  580.2 16.9 %collective-permute-start.13 = (f32[256,64]{0,1:T(8,128)S(1)}, f32[256,64]{0,1:T(8,128)S(1)}, u32[]{:S(2)}, u32[]{:S(2)}) collective-permute-start(f32[256,64]{0,1:T(8,128)S(1)} %fusion.224), channel_id=1, source_target_pairs={{32,0},{36,4},{40,8},{44,12},{48,16},{52,20},{56,24},{60,28},{64,3... | collective-permute-start | bytes 196616 | tf_op jit(solution)/shard_map/ppermute | solution.py:12
  592.7 17.0 %all-to-all-start.4 = ((f32[4,256,64]{1,2,0:T(8,128)}), f32[4,256,64]{1,2,0:T(8,128)S(1)}, u32[]{:S(2)}, u32[]{:S(2)}) async-start(f32[4,256,64]{1,2,0:T(8,128)} %stack.16), calls=%async_computation.4 | async-start | bytes 524288 | tf_op jit(solution)/shard_map/all_to_all | solution.py:103
  674.1 14.1 %collective-permute-start.29 = (f32[16,256]{1,0:T(8,128)S(1)}, f32[16,256]{1,0:T(8,128)S(1)}, u32[]{:S(2)}, u32[]{:S(2)}) collective-permute-start(f32[16,256]{1,0:T(8,128)S(1)} %fusion.222), channel_id=1, source_target_pairs={{64,0},{68,4},{72,8},{76,12},{80,16},{84,20},{88,24},{92,28},{96,3... | collective-permute-start | bytes 49160 | tf_op jit(solution)/shard_map/ppermute | solution.py:12
  678.7 9.8 %collective-permute-start.15 = (f32[256,256]{1,0:T(8,128)S(1)}, f32[256,256]{1,0:T(8,128)S(1)}, u32[]{:S(2)}, u32[]{:S(2)}) collective-permute-start(f32[256,256]{1,0:T(8,128)S(1)} %pad_maximum_fusion.7), channel_id=1, source_target_pairs={{64,0},{68,4},{72,8},{76,12},{80,16},{84,20},{88,24},{92,28},{96,3... | collective-permute-start | bytes 786440 | tf_op jit(solution)/shard_map/ppermute | solution.py:12
  683.1 17.8 %collective-permute-start.16 = (f32[256,64]{0,1:T(8,128)}, f32[256,64]{0,1:T(8,128)}, u32[]{:S(2)}, u32[]{:S(2)}) collective-permute-start(f32[256,64]{0,1:T(8,128)} %fusion.223), channel_id=1, source_target_pairs={{64,0},{68,4},{72,8},{76,12},{80,16},{84,20},{88,24},{92,28},{96,3... | collective-permute-start | bytes 196616 | tf_op jit(solution)/shard_map/ppermute | solution.py:12
  685.6 93.7 %collective-permute-start.28 = (f32[16,256]{1,0:T(8,128)}, f32[16,256]{1,0:T(8,128)S(1)}, u32[]{:S(2)}, u32[]{:S(2)}) collective-permute-start(f32[16,256]{1,0:T(8,128)} %fusion.253), channel_id=1, source_target_pairs={{0,64},{4,68},{8,72},{12,76},{16,80},{20,84},{24,88},{28,92},{32,9... | collective-permute-start | bytes 49160 | tf_op jit(solution)/shard_map/ppermute | solution.py:12
  696.4 17.9 %all-to-all-start.5 = ((f32[4,256,64]{1,2,0:T(8,128)}), f32[4,256,64]{1,2,0:T(8,128)S(1)}, u32[]{:S(2)}, u32[]{:S(2)}) async-start(f32[4,256,64]{1,2,0:T(8,128)} %stack.17), calls=%async_computation.5 | async-start | bytes 524288 | tf_op jit(solution)/shard_map/all_to_all | solution.py:103
  779.6 16.9 %collective-permute-start.31 = (f32[16,256]{1,0:T(8,128)S(1)}, f32[16,256]{1,0:T(8,128)S(1)}, u32[]{:S(2)}, u32[]{:S(2)}) collective-permute-start(f32[16,256]{1,0:T(8,128)S(1)} %fusion.211), channel_id=1, source_target_pairs={{128,0},{132,4},{136,8},{140,12},{144,16},{148,20},{152,24},{156,2... | collective-permute-start | bytes 49160 | tf_op jit(solution)/shard_map/ppermute | solution.py:12
  784.9 11.5 %collective-permute-start.30 = (f32[16,256]{1,0:T(8,128)S(1)}, f32[16,256]{1,0:T(8,128)S(1)}, u32[]{:S(2)}, u32[]{:S(2)}) collective-permute-start(f32[16,256]{1,0:T(8,128)S(1)} %fusion.255), channel_id=1, source_target_pairs={{0,128},{4,132},{8,136},{12,140},{16,144},{20,148},{24,152},{28,15... | collective-permute-start | bytes 49160 | tf_op jit(solution)/shard_map/ppermute | solution.py:12
  786.3 12.3 %collective-permute-start.18 = (f32[256,256]{1,0:T(8,128)S(1)}, f32[256,256]{1,0:T(8,128)S(1)}, u32[]{:S(2)}, u32[]{:S(2)}) collective-permute-start(f32[256,256]{1,0:T(8,128)S(1)} %pad_maximum_fusion.8), channel_id=1, source_target_pairs={{128,0},{132,4},{136,8},{140,12},{144,16},{148,20},{152,24},{156,2... | collective-permute-start | bytes 786440 | tf_op jit(solution)/shard_map/ppermute | solution.py:12
  795.2 10.8 %collective-permute-start.17 = (f32[256,64]{0,1:T(8,128)S(1)}, f32[256,64]{0,1:T(8,128)S(1)}, u32[]{:S(2)}, u32[]{:S(2)}) collective-permute-start(f32[256,64]{0,1:T(8,128)S(1)} %fusion.246), channel_id=1, source_target_pairs={{0,128},{4,132},{8,136},{12,140},{16,144},{20,148},{24,152},{28,15... | collective-permute-start | bytes 196616 | tf_op jit(solution)/shard_map/ppermute | solution.py:12
  (33 other events, 183.9 us)
